TPU v7x, 256 devices: a whole 4x4x8 slice. The times are simulated.
256 devices in a mesh: src: 2 (over y_lo), tx: 8 (over y_hi, x), ty: 16 (over z, core).
Axes of the slice: x: 4, y: 4 (y_hi: 2, y_lo: 2; y = y_hi * 2 + y_lo), z: 8, core: 2. Of those that a mesh axis runs over, the one named last changes fastest.
Arguments:
- orders: float32 [8, 2, 512, 512], P('src', None, 'tx', 'ty'), may hold values from -0.00390625 to 0.00390625
- offsets: int32 [8, 2], P('src'), may hold values from -8 to 7
- material: int32 [6, 2048, 2048], P(None, 'tx', 'ty'), may hold values from 0 to 3
- e_field: float32 [3, 6, 2048, 2048], P(None, None, 'tx', 'ty'), may hold values from -6 to 6
- h_field: float32 [3, 6, 2048, 2048], P(None, None, 'tx', 'ty'), may hold values from -6 to 6
Outputs:
- e_out: float32 [3, 6, 2048, 2048], P(None, None, 'tx', 'ty')
- h_out: float32 [3, 6, 2048, 2048], P(None, None, 'tx', 'ty')
All inputs are finite; a program needn't handle non-finite values.
Results may differ from a plain program's by a relative error of at most 0.0003.
Values sent between devices are 32-bit elements; how exact they have to be, the bound alone decides.
A program may use at most 128 MiB of HBM per device.

v0:
```python
import math
import jax
import jax.numpy as jnp
from jax import lax
from jax.sharding import PartitionSpec as P

STEPS = 4
ZINJ = 1
COURANT = 0.5
OMEGA = 0.7
PERMITTIVITY = (1.0, 2.6, 11.9, 2.1)
PREC = lax.Precision.HIGH
SPLIT = 32


def passed_along(block, axis, distance):
    devices = range(lax.axis_size(axis))
    route = [((i - distance) % len(devices), i) for i in devices]
    return lax.ppermute(block, axis, route)


def phase_tables(freqs, positions, length):
    product = jnp.mod(freqs[:, None] * positions[None, :], length)
    angle = product.astype(jnp.float32) * (2.0 * math.pi / length)
    return (jnp.cos(angle), jnp.sin(angle))


def base_tables(orders_n, positions, length):
    hi = jnp.arange(orders_n // SPLIT, dtype=jnp.int32) * SPLIT
    lo = jnp.arange(SPLIT, dtype=jnp.int32) - orders_n // 2
    c1, s1 = phase_tables(hi, positions, length)
    c2, s2 = phase_tables(lo, positions, length)
    cos_t = c1[:, None, :] * c2[None, :, :] - s1[:, None, :] * s2[None, :, :]
    sin_t = s1[:, None, :] * c2[None, :, :] + c1[:, None, :] * s2[None, :, :]
    return (cos_t.reshape(orders_n, -1), sin_t.reshape(orders_n, -1))


def cell_coefficient(material):
    total = jnp.zeros(material.shape, jnp.float32)
    for number in range(len(PERMITTIVITY)):
        total = total + jnp.where(material == number, COURANT / PERMITTIVITY[number], 0.0)
    return total


def fwd(field, axis):
    if axis == 0:
        zero = jnp.zeros((1,) + field.shape[1:], jnp.float32)
        return jnp.concatenate([field[1:], zero], 0) - field
    return jnp.roll(field, -1, axis) - field


def bwd(field, axis):
    if axis == 0:
        zero = jnp.zeros((1,) + field.shape[1:], jnp.float32)
        return field - jnp.concatenate([zero, field[:-1]], 0)
    return field - jnp.roll(field, 1, axis)


def injection_plane(orders, offsets, cells_x, cells_y):
    points, _, rows_kx, cols_ky = orders.shape
    n_tx = lax.axis_size("tx")
    n_ty = lax.axis_size("ty")
    full_x = cells_x * n_tx
    full_y = cells_y * n_ty
    mx = rows_kx * n_tx
    my = cols_ky * n_ty
    amp = lax.all_gather(orders, "ty", axis=3, tiled=True)
    a_re = amp[:, 0]
    a_im = amp[:, 1]
    y_pos = lax.axis_index("ty") * cells_y + jnp.arange(cells_y, dtype=jnp.int32)
    by_c, by_s = base_tables(my, y_pos, full_y)
    sy_c, sy_s = phase_tables(offsets[:, 1], y_pos, full_y)
    m_re = jnp.einsum("pkj,jy->pky", a_re, by_c, precision=PREC) - jnp.einsum(
        "pkj,jy->pky", a_im, by_s, precision=PREC
    )
    m_im = jnp.einsum("pkj,jy->pky", a_re, by_s, precision=PREC) + jnp.einsum(
        "pkj,jy->pky", a_im, by_c, precision=PREC
    )
    sy_c = sy_c[:, None, :]
    sy_s = sy_s[:, None, :]
    inner = jnp.stack([m_re * sy_c - m_im * sy_s, m_re * sy_s + m_im * sy_c], 1)
    inner = lax.all_gather(inner, "tx", axis=2, tiled=True)
    i_re = inner[:, 0]
    i_im = inner[:, 1]
    x_pos = lax.axis_index("tx") * cells_x + jnp.arange(cells_x, dtype=jnp.int32)
    bx_c, bx_s = base_tables(mx, x_pos, full_x)
    sx_c, sx_s = phase_tables(offsets[:, 0], x_pos, full_x)
    q_re = jnp.einsum("kx,pky->pxy", bx_c, i_re, precision=PREC) - jnp.einsum(
        "kx,pky->pxy", bx_s, i_im, precision=PREC
    )
    q_im = jnp.einsum("kx,pky->pxy", bx_c, i_im, precision=PREC) + jnp.einsum(
        "kx,pky->pxy", bx_s, i_re, precision=PREC
    )
    sx_c = sx_c[:, :, None]
    sx_s = sx_s[:, :, None]
    plane = jnp.stack(
        [jnp.sum(q_re * sx_c - q_im * sx_s, 0), jnp.sum(q_re * sx_s + q_im * sx_c, 0)]
    )
    return lax.psum(plane, "src")


def with_halo(stack, depth):
    ahead = passed_along(stack[:, :depth], "tx", -1)
    behind = passed_along(stack[:, -depth:], "tx", 1)
    stack = jnp.concatenate([stack, ahead, behind], 1)
    ahead = passed_along(jnp.swapaxes(stack[:, :, :depth], 1, 2), "ty", -1)
    behind = passed_along(jnp.swapaxes(stack[:, :, -depth:], 1, 2), "ty", 1)
    return jnp.concatenate([stack, jnp.swapaxes(ahead, 1, 2), jnp.swapaxes(behind, 1, 2)], 2)


def per_device(orders, offsets, material, e_field, h_field):
    layers, cells_x, cells_y = material.shape
    plane = injection_plane(orders, offsets, cells_x, cells_y)
    coefficient = cell_coefficient(material)
    stack = jnp.concatenate(
        [
            e_field.reshape(3 * layers, cells_x, cells_y),
            h_field.reshape(3 * layers, cells_x, cells_y),
            coefficient,
            plane,
        ],
        0,
    )
    ext = with_halo(stack, STEPS)
    n = 3 * layers
    e_x, e_y, e_z = (ext[i * layers : (i + 1) * layers] for i in range(3))
    h_x, h_y, h_z = (ext[n + i * layers : n + (i + 1) * layers] for i in range(3))
    coefficient = ext[2 * n : 2 * n + layers]
    plane_re = ext[2 * n + layers]
    plane_im = ext[2 * n + layers + 1]
    for step in range(STEPS):
        h_x = h_x - COURANT * (fwd(e_z, 2) - fwd(e_y, 0))
        h_y = h_y - COURANT * (fwd(e_x, 0) - fwd(e_z, 1))
        h_z = h_z - COURANT * (fwd(e_y, 1) - fwd(e_x, 2))
        e_x = e_x + coefficient * (bwd(h_z, 2) - bwd(h_y, 0))
        e_y = e_y + coefficient * (bwd(h_x, 0) - bwd(h_z, 1))
        e_z = e_z + coefficient * (bwd(h_y, 1) - bwd(h_x, 2))
        cosine = math.cos(OMEGA * (step + 1))
        sine = math.sin(OMEGA * (step + 1))
        e_x = e_x.at[ZINJ].add(COURANT * (cosine * plane_re - sine * plane_im))
        e_y = e_y.at[ZINJ].add(COURANT * (sine * plane_re + cosine * plane_im))
    crop = lambda f: f[:, :cells_x, :cells_y]
    return (
        jnp.stack([crop(e_x), crop(e_y), crop(e_z)]),
        jnp.stack([crop(h_x), crop(h_y), crop(h_z)]),
    )


def solution(mesh):
    in_specs = (
        P("src", None, "tx", "ty"),
        P("src", None),
        P(None, "tx", "ty"),
        P(None, None, "tx", "ty"),
        P(None, None, "tx", "ty"),
    )
    out_specs = (P(None, None, "tx", "ty"), P(None, None, "tx", "ty"))
    return jax.shard_map(
        per_device, mesh=mesh, in_specs=in_specs, out_specs=out_specs, check_vma=False
    )
```

profile of v0, /device:TPU:1, one launch (start us, length us, event | category | flops | bytes accessed | tf_op | source)
XLA Modules:
  0.0 297.1 jit_solution(6683656501134292388)
XLA Ops:
  10.9 43.5 %all-gather.3.cloned.1.call-done = f32[4,2,64,512]{2,0,1,3:T(4,128)} async-done(((f32[4,2,64,32]{2,0,1,3:T(4,128)}), f32[4,2,64,512]{2,0,1,3:T(4,128)}) %all-gather.3.cloned.1.call-update) | async-done | bytes 1048592 | tf_op jit(solution)/shard_map/all_gather | solution.py:67
  60.0 56.0 %all-gather.5.cloned.1.call-done = f32[4,2,512,128]{3,2,0,1:T(8,128)} async-done(((f32[4,2,64,128]{3,2,0,1:T(8,128)}), f32[4,2,512,128]{3,2,0,1:T(8,128)}) %all-gather.5.cloned.1.call-update) | async-done | bytes 2097168 | tf_op jit(solution)/shard_map/all_gather | solution.py:82
  116.0 2.4 fusion.75
  123.7 33.4 %all-reduce.18.cloned.1.call-done = f32[2,256,128]{1,2,0:T(8,128)} async-done(((f32[2,256,128]{1,2,0:T(8,128)}), f32[2,256,128]{1,2,0:T(8,128)}) %all-reduce.18.cloned.1.call-update) | async-done | bytes 262160 | tf_op jit(solution)/shard_map/psum | solution.py:99
  159.3 4.6 %collective-permute-start = (f32[44,4,128]{2,1,0:T(4,128)S(1)}, f32[44,4,128]{2,1,0:T(4,128)S(1)}, u32[]{:S(2)}, u32[]{:S(2)}) collective-permute-start(f32[44,4,128]{2,1,0:T(4,128)S(1)} %get-tuple-element.134), channel_id=1, source_target_pairs={{16,0},{32,16},{48,32},{64,48},{80,64},{96,80},{112,96},{0,112},{1... | collective-permute-start | bytes 270344 | tf_op jit(solution)/shard_map/ppermute | solution.py:19
  165.5 5.4 %collective-permute-done.1 = f32[44,4,128]{2,1,0:T(4,128)S(1)} collective-permute-done((f32[44,4,128]{2,1,0:T(4,128)S(1)}, f32[44,4,128]{2,1,0:T(4,128)S(1)}, u32[]{:S(2)}, u32[]{:S(2)}) %collective-permute-start.1) | collective-permute-done | bytes 90144 | tf_op jit(solution)/shard_map/ppermute | solution.py:19
  170.9 2.1 pad_maximum_fusion.1
  173.0 6.2 %slice_bitcast_fusion.1 = (f32[44,4,264]{1,2,0:T(8,128)}, f32[44,4,264]{1,2,0:T(8,128)}) fusion(f32[44,264,128]{2,1,0:T(8,128)S(1)} %pad_maximum_fusion.1), kind=kLoop, calls=%fused_computation.2 | loop fusion | bytes 743424 | tf_op jit(solution)/shard_map/transpose | solution.py:106
  179.2 5.5 %copy.35 = f32[44,4,264]{2,1,0:T(4,128)} copy(f32[44,4,264]{1,2,0:T(8,128)} %get-tuple-element.132) | data formatting | bytes 371712 | tf_op jit(solution)/shard_map/transpose | solution.py:106
  184.8 2.6 collective-permute-start.2
  187.3 5.5 %copy.37 = f32[44,4,264]{2,1,0:T(4,128)} copy(f32[44,4,264]{1,2,0:T(8,128)} %get-tuple-element.133) | data formatting | bytes 371712 | tf_op jit(solution)/shard_map/transpose | solution.py:107
  194.0 4.8 %copy.36 = f32[44,4,264]{1,2,0:T(8,128)} copy(f32[44,4,264]{2,1,0:T(4,128)} %collective-permute-done.2) | data formatting | bytes 371712 | tf_op jit(solution)/shard_map/ppermute | solution.py:19
  198.8 4.9 %copy.38 = f32[44,4,264]{1,2,0:T(8,128)} copy(f32[44,4,264]{2,1,0:T(4,128)} %collective-permute-done.3) | data formatting | bytes 371712 | tf_op jit(solution)/shard_map/ppermute | solution.py:19
  203.7 7.5 %pad_maximum_fusion = f32[44,264,136]{2,1,0:T(8,128)S(1)} fusion(f32[44,264,4]{2,1,0:T(8,128)} %bitcast.125, f32[44,264,4]{2,1,0:T(8,128)} %bitcast.124, f32[44,4,128]{2,1,0:T(4,128)} %copy-done.15, f32[44,4,128]{2,1,0:T(4,128)S(1)} %collective-permute-done, f32[2,256,128]{2,1,0:T(8,128)S(1)} %copy.34, f32[6,256,128]{2,1,0:T(8,128)S(1)} %select_add_fusion, ...), kind=kLoop, calls=%fused_computation | loop fusion | flops 11058432 | bytes 12638208 | tf_op jit(solution)/shard_map/concatenate | solution.py:108
  212.3 2.5 copy-done.3
  217.1 2.7 fusion.9
  221.5 2.3 fusion.17
  232.6 4.1 %fusion.20 = (f32[6,264,136]{2,1,0:T(8,128)S(1)}, f32[6,264,136]{2,1,0:T(8,128)S(1)}, f32[6,264,136]{2,1,0:T(8,128)S(1)}) fusion(f32[6,264,136]{2,1,0:T(8,128)S(1)} %get-tuple-element.122, f32[6,264,136]{2,1,0:T(8,128)S(1)} %get-tuple-element.120, f32[6,1,136]{2,1,0:T(1,128)S(1)} %slice.659, f32[6,263,136]{2,1,0:T(8,128)S(1)} %slice.658, ...), kind=kLoop, calls=%fused_computation.42 | loop fusion | flops 4093056 | bytes 12638208 | tf_op jit(solution)/shard_map/sub | solution.py:134
  241.5 3.5 %fusion.35 = (f32[6,264,136]{2,1,0:T(8,128)S(1)}, f32[6,264,136]{2,1,0:T(8,128)S(1)}, f32[6,264,136]{2,1,0:T(8,128)S(1)}) fusion(f32[6,264,136]{2,1,0:T(8,128)S(1)} %get-tuple-element.120, f32[6,264,136]{2,1,0:T(8,128)S(1)} %get-tuple-element.147, f32[6,263,136]{2,1,0:T(8,128)S(1)} %bitcast.108, f32[6,1,136]{2,1,0:T(1,128)S(1)} %slice.677, ...), kind=kLoop, calls=%fused_computation.64 | loop fusion | flops 4093056 | bytes 13499904 | tf_op jit(solution)/shard_map/add | solution.py:136
  253.1 4.1 %fusion.38 = (f32[6,264,136]{2,1,0:T(8,128)S(1)}, f32[6,264,136]{2,1,0:T(8,128)S(1)}, f32[6,264,136]{2,1,0:T(8,128)S(1)}) fusion(f32[6,264,136]{2,1,0:T(8,128)S(1)} %get-tuple-element.147, f32[6,264,136]{2,1,0:T(8,128)S(1)} %get-tuple-element.118, f32[6,1,136]{2,1,0:T(1,128)S(1)} %slice.681, f32[6,263,136]{2,1,0:T(8,128)S(1)} %slice.680, ...), kind=kLoop, calls=%fused_computation.68 | loop fusion | flops 4093056 | bytes 12638208 | tf_op jit(solution)/shard_map/sub | solution.py:134
  263.0 3.5 %fusion.53 = (f32[6,264,136]{2,1,0:T(8,128)S(1)}, f32[6,264,136]{2,1,0:T(8,128)S(1)}, f32[6,264,136]{2,1,0:T(8,128)S(1)}) fusion(f32[6,264,136]{2,1,0:T(8,128)S(1)} %get-tuple-element.118, f32[6,264,136]{2,1,0:T(8,128)S(1)} %get-tuple-element.144, f32[6,263,136]{2,1,0:T(8,128)S(1)} %bitcast.110, f32[6,1,136]{2,1,0:T(1,128)S(1)} %slice.699, ...), kind=kLoop, calls=%fused_computation.90 | loop fusion | flops 4093056 | bytes 13499904 | tf_op jit(solution)/shard_map/add | solution.py:136
  269.6 2.3 fusion.56
  276.5 5.5 %fusion.59 = (f32[6,264,136]{2,1,0:T(8,128)}, f32[6,264,136]{2,1,0:T(8,128)}, f32[6,264,136]{2,1,0:T(8,128)}) fusion(f32[6,264,136]{2,1,0:T(8,128)S(1)} %get-tuple-element.117, f32[6,264,136]{2,1,0:T(8,128)S(1)} %get-tuple-element.141, f32[6,264,135]{2,1,0:T(8,128)S(1)} %bitcast.117, f32[6,264,1]{2,1,0:T(8,128)} %slice.706, ...), kind=kLoop, calls=%fused_computation.99 | loop fusion | flops 2585088 | bytes 10914816 | tf_op jit(solution)/shard_map/add | solution.py:135
  282.0 2.1 fusion.87
  (139 shorter events, 65.8 us)
Async XLA Ops:
  7.2 47.2 %all-gather.3.cloned.1.call-start = ((), (), s32[]{:S(2)}) async-start(), calls=%async_computation | async-start | bytes 2228224 | tf_op jit(solution)/shard_map/all_gather | solution.py:67
  8.9 107.1 %all-gather.5.cloned.1.call-start = ((), (), s32[]{:S(2)}) async-start(), calls=%async_computation.1 | async-start | bytes 2359296 | tf_op jit(solution)/shard_map/all_gather | solution.py:82
  56.4 1.0 copy-start.14
  59.3 97.8 %all-reduce.18.cloned.1.call-start = ((), (), s32[]{:S(2)}) async-start(), calls=%async_computation.2 | async-start | bytes 524288 | tf_op jit(solution)/shard_map/psum | solution.py:99
  116.0 2.4 copy-start.11
  121.5 36.7 %copy-start.1 = (f32[3,6,256,128]{3,2,1,0:T(8,128)S(1)}, f32[3,6,256,128]{3,2,1,0:T(8,128)}, u32[]{:S(2)}) copy-start(f32[3,6,256,128]{3,2,1,0:T(8,128)} %param.25) | copy-start | bytes 7077892
  158.1 12.8 %copy-start.2 = (f32[3,6,256,128]{3,2,1,0:T(8,128)S(1)}, f32[3,6,256,128]{3,2,1,0:T(8,128)}, u32[]{:S(2)}) copy-start(f32[3,6,256,128]{3,2,1,0:T(8,128)} %param.24) | copy-start | bytes 7077892
  159.3 6.2 %collective-permute-start = (f32[44,4,128]{2,1,0:T(4,128)S(1)}, f32[44,4,128]{2,1,0:T(4,128)S(1)}, u32[]{:S(2)}, u32[]{:S(2)}) collective-permute-start(f32[44,4,128]{2,1,0:T(4,128)S(1)} %get-tuple-element.134), channel_id=1, source_target_pairs={{16,0},{32,16},{48,32},{64,48},{80,64},{96,80},{112,96},{0,112},{1... | collective-permute-start | bytes 270344 | tf_op jit(solution)/shard_map/ppermute | solution.py:19
  163.9 7.0 %collective-permute-start.1 = (f32[44,4,128]{2,1,0:T(4,128)S(1)}, f32[44,4,128]{2,1,0:T(4,128)S(1)}, u32[]{:S(2)}, u32[]{:S(2)}) collective-permute-start(f32[44,4,128]{2,1,0:T(4,128)S(1)} %get-tuple-element.135), channel_id=1, source_target_pairs={{112,0},{0,16},{16,32},{32,48},{48,64},{64,80},{80,96},{96,112},{1... | collective-permute-start | bytes 270344 | tf_op jit(solution)/shard_map/ppermute | solution.py:19
  170.9 2.1 copy-start.15
  184.8 9.2 %collective-permute-start.2 = (f32[44,4,264]{2,1,0:T(4,128)}, f32[44,4,264]{2,1,0:T(4,128)}, u32[]{:S(2)}, u32[]{:S(2)}) collective-permute-start(f32[44,4,264]{2,1,0:T(4,128)} %copy.35), channel_id=1, source_target_pairs={{1,0},{2,1},{3,2},{4,3},{5,4},{6,5},{7,6},{8,7},{9,8},{10,9},{11,1... | collective-permute-start | bytes 557576 | tf_op jit(solution)/shard_map/ppermute | solution.py:19
  192.8 6.0 %collective-permute-start.3 = (f32[44,4,264]{2,1,0:T(4,128)}, f32[44,4,264]{2,1,0:T(4,128)}, u32[]{:S(2)}, u32[]{:S(2)}) collective-permute-start(f32[44,4,264]{2,1,0:T(4,128)} %copy.37), channel_id=1, source_target_pairs={{15,0},{0,1},{1,2},{2,3},{3,4},{4,5},{5,6},{6,7},{7,8},{8,9},{9,10... | collective-permute-start | bytes 557576 | tf_op jit(solution)/shard_map/ppermute | solution.py:19
  211.2 55.4 %copy-start = (f32[44,264,136]{2,1,0:T(8,128)}, f32[44,264,136]{2,1,0:T(8,128)S(1)}, u32[]{:S(2)}) copy-start(f32[44,264,136]{2,1,0:T(8,128)S(1)} %pad_maximum_fusion) | copy-start | bytes 18957316
  211.4 3.4 %copy-start.3 = (f32[3,6,256,128]{3,2,1,0:T(8,128)S(1)}, f32[3,6,256,128]{3,2,1,0:T(8,128)}, u32[]{:S(2)}) copy-start(f32[3,6,256,128]{3,2,1,0:T(8,128)} %param.24) | copy-start | bytes 7077892
  211.4 3.4 %copy-start.16 = (f32[44,4,128]{2,1,0:T(4,128)S(1)}, f32[44,4,128]{2,1,0:T(4,128)}, u32[]{:S(2)}) copy-start(f32[44,4,128]{2,1,0:T(4,128)} %copy-done.15) | copy-start | bytes 270340
  219.8 1.2 copy-start.7
  220.1 1.4 copy-start.13
  230.6 2.0 copy-start.8
  257.3 2.7 copy-start.4
  261.1 1.9 copy-start.5
  268.1 1.4 copy-start.6
  271.9 1.5 copy-start.9
  274.6 1.9 copy-start.10
  284.1 1.6 copy-start.12
Sparse Core Ops, SparseCore 0:
  10.4 43.9 all-gather.2
  59.4 56.5 all-gather.4
  122.3 34.6 all-reduce.17
where the time goes:
time: 298 us; the launch traced here: 297 us
  waiting for transfers between devices  140 us (47%)
  local copies, waits for them, and re-layouts  75.9 us (25%)
  other arithmetic  51.6 us (17%)
  between operations  14.4 us (5%)
  starting transfers between devices  8.49 us (3%)
  matrix products  6.93 us (2%)
    all_gather x1, waiting for transfers between devices, injection_plane(): inner = lax.all_gather(inner, 'tx', axis=2, tiled=True)  56 us
    all_gather x1, waiting for transfers between devices, injection_plane(): amp = lax.all_gather(orders, 'ty', axis=3, tiled=True)  43.5 us
    psum x1, waiting for transfers between devices, injection_plane(): return lax.psum(plane, 'src')  33.4 us
    slice x27, local copies, waits for them, and re-layouts, fwd(): return jnp.roll(field, -1, axis) - field  15.9 us
    sub x4, other arithmetic, per_device(): h_z = h_z - COURANT * (fwd(e_y, 1) - fwd(e_x, 2))  13.2 us
    transpose x2, local copies, waits for them, and re-layouts, with_halo(): ahead = passed_along(jnp.swapaxes(stack[:, :, :depth], 1, 2), 'ty', -1)  11.7 us
    unnamed x37, local copies, waits for them, and re-layouts  9.9 us
    ppermute x2, local copies, waits for them, and re-layouts, passed_along(): return lax.ppermute(block, axis, route)  9.72 us
  transfers between devices with their start and end apart: 7, of which 5 were waited for; matrix products, arithmetic and copies ran while one was open for 5% of the time, Pallas kernels for 0%

commit v1 on v0

--- a/solution.py
+++ b/solution.py
@@ -79,7 +79,9 @@
     sy_c = sy_c[:, None, :]
     sy_s = sy_s[:, None, :]
     inner = jnp.stack([m_re * sy_c - m_im * sy_s, m_re * sy_s + m_im * sy_c], 1)
-    inner = lax.all_gather(inner, "tx", axis=2, tiled=True)
+    inner = jnp.concatenate(
+        lax.all_to_all(jnp.stack([inner] * lax.axis_size("tx")), "tx", 0, 0), axis=2
+    )
     i_re = inner[:, 0]
     i_im = inner[:, 1]
     x_pos = lax.axis_index("tx") * cells_x + jnp.arange(cells_x, dtype=jnp.int32)

time: 298 us -> 276 us (0.926)
  waiting for transfers between devices: 140 us -> 111 us
  starting transfers between devices: 8.49 us -> 14.9 us
    all_gather x1 -> x0, waiting for transfers between devices: 56 us -> none  [injection_plane(): inner = lax.all_gather(inner, 'tx', axis=2, tiled=True)]
    all_to_all x0 -> x1, waiting for transfers between devices: none -> 27.9 us  [injection_plane(): lax.all_to_all(jnp.stack([inner] * lax.axis_size('tx')), 'tx', 0, 0)]
    all_to_all x0 -> x1, starting transfers between devices: none -> 6.42 us  [injection_plane(): lax.all_to_all(jnp.stack([inner] * lax.axis_size('tx')), 'tx', 0, 0)]
    unnamed x37 -> x35, local copies, waits for them, and re-layouts: 9.9 us -> 9.92 us
where the time goes in v1:
time: 276 us; the launch traced here: 275 us
  waiting for transfers between devices  111 us (40%)
  local copies, waits for them, and re-layouts  77.7 us (28%)
  other arithmetic  50.9 us (18%)
  starting transfers between devices  14.9 us (5%)
  between operations  14.7 us (5%)
  matrix products  5.65 us (2%)
    all_gather x1, waiting for transfers between devices, injection_plane(): amp = lax.all_gather(orders, 'ty', axis=3, tiled=True)  43.5 us
    psum x1, waiting for transfers between devices, injection_plane(): return lax.psum(plane, 'src')  32.6 us
    all_to_all x1, waiting for transfers between devices, injection_plane(): lax.all_to_all(jnp.stack([inner] * lax.axis_size('tx')), 'tx', 0, 0)  27.9 us
    slice x27, local copies, waits for them, and re-layouts, fwd(): return jnp.roll(field, -1, axis) - field  15.8 us
    sub x4, other arithmetic, per_device(): h_z = h_z - COURANT * (fwd(e_y, 1) - fwd(e_x, 2))  13.2 us
    transpose x2, local copies, waits for them, and re-layouts, with_halo(): ahead = passed_along(jnp.swapaxes(stack[:, :, :depth], 1, 2), 'ty', -1)  11.7 us
    unnamed x35, local copies, waits for them, and re-layouts  9.92 us
    ppermute x2, local copies, waits for them, and re-layouts, passed_along(): return lax.ppermute(block, axis, route)  9.72 us
  transfers between devices with their start and end apart: 7, of which 5 were waited for; matrix products, arithmetic and copies ran while one was open for 5% of the time, Pallas kernels for 0%

profile of v1, /device:TPU:1, one launch (start us, length us, event | category | flops | bytes accessed | tf_op | source)
XLA Modules:
  0.0 274.8 jit_solution(2315649546439868994)
XLA Ops:
  10.9 43.5 %all-gather.2.cloned.1.call-done = f32[4,2,64,512]{2,0,1,3:T(4,128)} async-done(((f32[4,2,64,32]{2,0,1,3:T(4,128)}), f32[4,2,64,512]{2,0,1,3:T(4,128)}) %all-gather.2.cloned.1.call-update) | async-done | bytes 1048592 | tf_op jit(solution)/shard_map/all_gather | solution.py:67
  60.2 6.4 %all-to-all-start = ((f32[8,4,2,64,128]{4,3,2,1,0:T(8,128)}), f32[8,4,2,64,128]{4,3,2,1,0:T(8,128)S(1)}, u32[]{:S(2)}, u32[]{:S(2)}) async-start(f32[8,4,2,64,128]{4,3,2,1,0:T(8,128)} %stack.56), calls=%async_computation | async-start | bytes 4194304 | tf_op jit(solution)/shard_map/all_to_all | solution.py:83
  67.3 27.9 %all-to-all-done = f32[8,4,2,64,128]{4,3,2,1,0:T(8,128)S(1)} async-done(((f32[8,4,2,64,128]{4,3,2,1,0:T(8,128)}), f32[8,4,2,64,128]{4,3,2,1,0:T(8,128)S(1)}, u32[]{:S(2)}, u32[]{:S(2)}) %all-to-all-start) | async-done | bytes 2097184 | tf_op jit(solution)/shard_map/all_to_all | solution.py:83
  101.8 32.6 %all-reduce.18.cloned.1.call-done = f32[2,256,128]{1,2,0:T(8,128)} async-done(((f32[2,256,128]{1,2,0:T(8,128)}), f32[2,256,128]{1,2,0:T(8,128)}) %all-reduce.18.cloned.1.call-update) | async-done | bytes 262160 | tf_op jit(solution)/shard_map/psum | solution.py:101
  136.6 4.6 %collective-permute-start = (f32[44,4,128]{2,1,0:T(4,128)S(1)}, f32[44,4,128]{2,1,0:T(4,128)S(1)}, u32[]{:S(2)}, u32[]{:S(2)}) collective-permute-start(f32[44,4,128]{2,1,0:T(4,128)S(1)} %get-tuple-element.134), channel_id=1, source_target_pairs={{16,0},{32,16},{48,32},{64,48},{80,64},{96,80},{112,96},{0,112},{1... | collective-permute-start | bytes 270344 | tf_op jit(solution)/shard_map/ppermute | solution.py:19
  142.8 5.4 %collective-permute-done.1 = f32[44,4,128]{2,1,0:T(4,128)S(1)} collective-permute-done((f32[44,4,128]{2,1,0:T(4,128)S(1)}, f32[44,4,128]{2,1,0:T(4,128)S(1)}, u32[]{:S(2)}, u32[]{:S(2)}) %collective-permute-start.1) | collective-permute-done | bytes 90144 | tf_op jit(solution)/shard_map/ppermute | solution.py:19
  148.3 2.1 pad_maximum_fusion.1
  150.4 6.2 %slice_bitcast_fusion.1 = (f32[44,4,264]{1,2,0:T(8,128)}, f32[44,4,264]{1,2,0:T(8,128)}) fusion(f32[44,264,128]{2,1,0:T(8,128)S(1)} %pad_maximum_fusion.1), kind=kLoop, calls=%fused_computation.2 | loop fusion | bytes 743424 | tf_op jit(solution)/shard_map/transpose | solution.py:108
  156.6 5.5 %copy.36 = f32[44,4,264]{2,1,0:T(4,128)} copy(f32[44,4,264]{1,2,0:T(8,128)} %get-tuple-element.132) | data formatting | bytes 371712 | tf_op jit(solution)/shard_map/transpose | solution.py:108
  162.1 2.6 collective-permute-start.2
  164.7 5.5 %copy.38 = f32[44,4,264]{2,1,0:T(4,128)} copy(f32[44,4,264]{1,2,0:T(8,128)} %get-tuple-element.133) | data formatting | bytes 371712 | tf_op jit(solution)/shard_map/transpose | solution.py:109
  171.3 4.8 %copy.37 = f32[44,4,264]{1,2,0:T(8,128)} copy(f32[44,4,264]{2,1,0:T(4,128)} %collective-permute-done.2) | data formatting | bytes 371712 | tf_op jit(solution)/shard_map/ppermute | solution.py:19
  176.2 4.9 %copy.39 = f32[44,4,264]{1,2,0:T(8,128)} copy(f32[44,4,264]{2,1,0:T(4,128)} %collective-permute-done.3) | data formatting | bytes 371712 | tf_op jit(solution)/shard_map/ppermute | solution.py:19
  181.1 7.5 %pad_maximum_fusion = f32[44,264,136]{2,1,0:T(8,128)S(1)} fusion(f32[44,264,4]{2,1,0:T(8,128)} %bitcast.132, f32[44,264,4]{2,1,0:T(8,128)} %bitcast.131, f32[44,4,128]{2,1,0:T(4,128)} %copy-done.14, f32[44,4,128]{2,1,0:T(4,128)S(1)} %collective-permute-done, f32[2,256,128]{2,1,0:T(8,128)S(1)} %copy.35, f32[6,256,128]{2,1,0:T(8,128)S(1)} %select_add_fusion, ...), kind=kLoop, calls=%fused_computation | loop fusion | flops 11058432 | bytes 12638208 | tf_op jit(solution)/shard_map/concatenate | solution.py:110
  189.7 2.5 copy-done.3
  194.5 2.7 fusion.9
  198.9 2.3 fusion.17
  210.0 4.1 %fusion.20 = (f32[6,264,136]{2,1,0:T(8,128)S(1)}, f32[6,264,136]{2,1,0:T(8,128)S(1)}, f32[6,264,136]{2,1,0:T(8,128)S(1)}) fusion(f32[6,264,136]{2,1,0:T(8,128)S(1)} %get-tuple-element.122, f32[6,264,136]{2,1,0:T(8,128)S(1)} %get-tuple-element.120, f32[6,1,136]{2,1,0:T(1,128)S(1)} %slice.659, f32[6,263,136]{2,1,0:T(8,128)S(1)} %slice.658, ...), kind=kLoop, calls=%fused_computation.42 | loop fusion | flops 4093056 | bytes 12638208 | tf_op jit(solution)/shard_map/sub | solution.py:136
  218.9 3.5 %fusion.35 = (f32[6,264,136]{2,1,0:T(8,128)S(1)}, f32[6,264,136]{2,1,0:T(8,128)S(1)}, f32[6,264,136]{2,1,0:T(8,128)S(1)}) fusion(f32[6,264,136]{2,1,0:T(8,128)S(1)} %get-tuple-element.120, f32[6,264,136]{2,1,0:T(8,128)S(1)} %get-tuple-element.147, f32[6,263,136]{2,1,0:T(8,128)S(1)} %bitcast.115, f32[6,1,136]{2,1,0:T(1,128)S(1)} %slice.677, ...), kind=kLoop, calls=%fused_computation.64 | loop fusion | flops 4093056 | bytes 13499904 | tf_op jit(solution)/shard_map/add | solution.py:138
  230.5 4.1 %fusion.38 = (f32[6,264,136]{2,1,0:T(8,128)S(1)}, f32[6,264,136]{2,1,0:T(8,128)S(1)}, f32[6,264,136]{2,1,0:T(8,128)S(1)}) fusion(f32[6,264,136]{2,1,0:T(8,128)S(1)} %get-tuple-element.147, f32[6,264,136]{2,1,0:T(8,128)S(1)} %get-tuple-element.118, f32[6,1,136]{2,1,0:T(1,128)S(1)} %slice.681, f32[6,263,136]{2,1,0:T(8,128)S(1)} %slice.680, ...), kind=kLoop, calls=%fused_computation.68 | loop fusion | flops 4093056 | bytes 12638208 | tf_op jit(solution)/shard_map/sub | solution.py:136
  240.4 3.5 %fusion.53 = (f32[6,264,136]{2,1,0:T(8,128)S(1)}, f32[6,264,136]{2,1,0:T(8,128)S(1)}, f32[6,264,136]{2,1,0:T(8,128)S(1)}) fusion(f32[6,264,136]{2,1,0:T(8,128)S(1)} %get-tuple-element.118, f32[6,264,136]{2,1,0:T(8,128)S(1)} %get-tuple-element.144, f32[6,263,136]{2,1,0:T(8,128)S(1)} %bitcast.117, f32[6,1,136]{2,1,0:T(1,128)S(1)} %slice.699, ...), kind=kLoop, calls=%fused_computation.90 | loop fusion | flops 4093056 | bytes 13499904 | tf_op jit(solution)/shard_map/add | solution.py:138
  246.9 2.3 fusion.56
  253.9 5.5 %fusion.59 = (f32[6,264,136]{2,1,0:T(8,128)}, f32[6,264,136]{2,1,0:T(8,128)}, f32[6,264,136]{2,1,0:T(8,128)}) fusion(f32[6,264,136]{2,1,0:T(8,128)S(1)} %get-tuple-element.117, f32[6,264,136]{2,1,0:T(8,128)S(1)} %get-tuple-element.141, f32[6,264,135]{2,1,0:T(8,128)S(1)} %bitcast.124, f32[6,264,1]{2,1,0:T(8,128)} %slice.706, ...), kind=kLoop, calls=%fused_computation.99 | loop fusion | flops 2585088 | bytes 10914816 | tf_op jit(solution)/shard_map/add | solution.py:137
  259.3 2.1 fusion.87
  (139 shorter events, 68.0 us)
Async XLA Ops:
  7.2 47.2 %all-gather.2.cloned.1.call-start = ((), (), s32[]{:S(2)}) async-start(), calls=%async_computation.1 | async-start | bytes 2228224 | tf_op jit(solution)/shard_map/all_gather | solution.py:67
  56.4 1.0 copy-start.13
  60.2 35.0 %all-to-all-start = ((f32[8,4,2,64,128]{4,3,2,1,0:T(8,128)}), f32[8,4,2,64,128]{4,3,2,1,0:T(8,128)S(1)}, u32[]{:S(2)}, u32[]{:S(2)}) async-start(f32[8,4,2,64,128]{4,3,2,1,0:T(8,128)} %stack.56), calls=%async_computation | async-start | bytes 4194304 | tf_op jit(solution)/shard_map/all_to_all | solution.py:83
  66.6 67.8 %all-reduce.18.cloned.1.call-start = ((), (), s32[]{:S(2)}) async-start(), calls=%async_computation.2 | async-start | bytes 524288 | tf_op jit(solution)/shard_map/psum | solution.py:101
  99.6 35.9 %copy-start.1 = (f32[3,6,256,128]{3,2,1,0:T(8,128)S(1)}, f32[3,6,256,128]{3,2,1,0:T(8,128)}, u32[]{:S(2)}) copy-start(f32[3,6,256,128]{3,2,1,0:T(8,128)} %param.25) | copy-start | bytes 7077892
  135.5 12.8 %copy-start.2 = (f32[3,6,256,128]{3,2,1,0:T(8,128)S(1)}, f32[3,6,256,128]{3,2,1,0:T(8,128)}, u32[]{:S(2)}) copy-start(f32[3,6,256,128]{3,2,1,0:T(8,128)} %param.24) | copy-start | bytes 7077892
  136.6 6.2 %collective-permute-start = (f32[44,4,128]{2,1,0:T(4,128)S(1)}, f32[44,4,128]{2,1,0:T(4,128)S(1)}, u32[]{:S(2)}, u32[]{:S(2)}) collective-permute-start(f32[44,4,128]{2,1,0:T(4,128)S(1)} %get-tuple-element.134), channel_id=1, source_target_pairs={{16,0},{32,16},{48,32},{64,48},{80,64},{96,80},{112,96},{0,112},{1... | collective-permute-start | bytes 270344 | tf_op jit(solution)/shard_map/ppermute | solution.py:19
  141.3 7.0 %collective-permute-start.1 = (f32[44,4,128]{2,1,0:T(4,128)S(1)}, f32[44,4,128]{2,1,0:T(4,128)S(1)}, u32[]{:S(2)}, u32[]{:S(2)}) collective-permute-start(f32[44,4,128]{2,1,0:T(4,128)S(1)} %get-tuple-element.135), channel_id=1, source_target_pairs={{112,0},{0,16},{16,32},{32,48},{48,64},{64,80},{80,96},{96,112},{1... | collective-permute-start | bytes 270344 | tf_op jit(solution)/shard_map/ppermute | solution.py:19
  148.3 2.1 copy-start.14
  162.1 9.2 %collective-permute-start.2 = (f32[44,4,264]{2,1,0:T(4,128)}, f32[44,4,264]{2,1,0:T(4,128)}, u32[]{:S(2)}, u32[]{:S(2)}) collective-permute-start(f32[44,4,264]{2,1,0:T(4,128)} %copy.36), channel_id=1, source_target_pairs={{1,0},{2,1},{3,2},{4,3},{5,4},{6,5},{7,6},{8,7},{9,8},{10,9},{11,1... | collective-permute-start | bytes 557576 | tf_op jit(solution)/shard_map/ppermute | solution.py:19
  170.2 6.0 %collective-permute-start.3 = (f32[44,4,264]{2,1,0:T(4,128)}, f32[44,4,264]{2,1,0:T(4,128)}, u32[]{:S(2)}, u32[]{:S(2)}) collective-permute-start(f32[44,4,264]{2,1,0:T(4,128)} %copy.38), channel_id=1, source_target_pairs={{15,0},{0,1},{1,2},{2,3},{3,4},{4,5},{5,6},{6,7},{7,8},{8,9},{9,10... | collective-permute-start | bytes 557576 | tf_op jit(solution)/shard_map/ppermute | solution.py:19
  188.6 55.4 %copy-start = (f32[44,264,136]{2,1,0:T(8,128)}, f32[44,264,136]{2,1,0:T(8,128)S(1)}, u32[]{:S(2)}) copy-start(f32[44,264,136]{2,1,0:T(8,128)S(1)} %pad_maximum_fusion) | copy-start | bytes 18957316
  188.8 3.4 %copy-start.3 = (f32[3,6,256,128]{3,2,1,0:T(8,128)S(1)}, f32[3,6,256,128]{3,2,1,0:T(8,128)}, u32[]{:S(2)}) copy-start(f32[3,6,256,128]{3,2,1,0:T(8,128)} %param.24) | copy-start | bytes 7077892
  188.8 3.4 %copy-start.15 = (f32[44,4,128]{2,1,0:T(4,128)S(1)}, f32[44,4,128]{2,1,0:T(4,128)}, u32[]{:S(2)}) copy-start(f32[44,4,128]{2,1,0:T(4,128)} %copy-done.14) | copy-start | bytes 270340
  197.2 1.2 copy-start.7
  197.5 1.4 copy-start.12
  208.0 2.0 copy-start.8
  234.6 2.7 copy-start.4
  238.5 1.9 copy-start.5
  245.5 1.4 copy-start.6
  249.2 1.5 copy-start.9
  252.0 1.9 copy-start.10
  261.4 1.6 copy-start.11
Sparse Core Ops, SparseCore 0:
  10.4 43.9 all-gather.1
  100.5 33.8 all-reduce.17
